TPU v7x, 32 devices: a whole 2x2x4 slice. The times are simulated.
32 devices in a mesh: seq: 4 (over y, x), vocab: 8 (over z, core).
Axes of the slice: x: 2, y: 2, z: 4, core: 2. Of those that a mesh axis runs over, the one named last changes fastest.
Arguments:
- teacher_hidden: bfloat16 [1024, 8192], P(None, 'seq'), may hold values from -480 to 480
- teacher_head: bfloat16 [8192, 81920], P('seq', 'vocab'), may hold values from -1 to 1
- student_hidden: bfloat16 [1024, 3584], P(None, 'seq'), may hold values from -480 to 480
- student_head: bfloat16 [3584, 81920], P('seq', 'vocab'), may hold values from -1 to 1
- kept: int32 [8, 64], replicated, may hold values from 0 to 639, as said below
Outputs:
- loss_rows: float32 [1024], P('seq')
- hidden_grad: bfloat16 [1024, 3584], P('vocab', 'seq')
- head_grad: bfloat16 [3584, 81920], P('seq', 'vocab')
Inputs may be any that keep to these rules, and one draw needn't show every extreme that they name: `kept`: each row holds 64 distinct block ids in ascending order. In every row at most 8 of them lie within one run of 80 consecutive blocks starting at a multiple of 80, and in every row some such run holds exactly 8.
All inputs are finite; a program needn't handle non-finite values.
Results may differ from a plain program's by a relative error of at most 0.0049.
Values may be sent and summed in bfloat16 or wider, within the bound.
A program may use at most 256 MiB of HBM per device.

v0:
```python
import jax
import jax.numpy as jnp
from jax import lax
from jax.experimental import pallas as pl
from jax.experimental.pallas import tpu as pltpu
from jax.sharding import PartitionSpec as P


BLOCK = 128

masked_value = -1e30
loss_scale = 2048.0


def kept_kernel(ids_ref, hidden_ref, head_ref, out_ref):
    out_ref[...] = jnp.dot(
        hidden_ref[...], head_ref[...], preferred_element_type=jnp.float32
    )


def kept_partials(ids, hidden, head):
    row_blocks, slots = ids.shape
    depth = hidden.shape[1]
    return pl.pallas_call(
        kept_kernel,
        out_shape=jax.ShapeDtypeStruct((row_blocks * BLOCK, slots * BLOCK), jnp.float32),
        grid_spec=pltpu.PrefetchScalarGridSpec(
            num_scalar_prefetch=1,
            grid=(row_blocks, slots),
            in_specs=[
                pl.BlockSpec((BLOCK, depth), lambda r, m, ids: (r, 0)),
                pl.BlockSpec((depth, BLOCK), lambda r, m, ids: (0, ids[r, m])),
            ],
            out_specs=pl.BlockSpec((BLOCK, BLOCK), lambda r, m, ids: (r, m)),
        ),
        cost_estimate=pl.CostEstimate(
            flops=2 * row_blocks * slots * BLOCK * BLOCK * depth,
            bytes_accessed=2 * row_blocks * slots * BLOCK * depth,
            transcendentals=0,
        ),
        name="kept_partials",
    )(ids, hidden, head)


TILE = 512


def columns_kernel(offset_ref, left_ref, right_ref, *rest):
    rest[-1][...] = jnp.dot(
        left_ref[...], right_ref[...], preferred_element_type=jnp.float32
    ).astype(jnp.bfloat16)


def put_columns(left, right, whole, cols, owner):
    rows, depth = left.shape
    part = right.shape[1]
    tiles = part // TILE
    offset = (owner * tiles).astype(jnp.int32).reshape(1)
    in_specs = [
        pl.BlockSpec((rows, depth), lambda j, o: (0, 0)),
        pl.BlockSpec((depth, TILE), lambda j, o: (0, j)),
    ]
    operands = [offset, left, right]
    aliases = {}
    if whole is not None:
        in_specs.append(pl.BlockSpec(memory_space=pl.ANY))
        operands.append(whole)
        aliases = {3: 0}
    return pl.pallas_call(
        columns_kernel,
        out_shape=jax.ShapeDtypeStruct((rows, cols), jnp.bfloat16),
        grid_spec=pltpu.PrefetchScalarGridSpec(
            num_scalar_prefetch=1,
            grid=(tiles,),
            in_specs=in_specs,
            out_specs=pl.BlockSpec((rows, TILE), lambda j, o: (0, o[0] + j)),
        ),
        input_output_aliases=aliases,
        cost_estimate=pl.CostEstimate(
            flops=2 * rows * depth * part,
            bytes_accessed=2 * (rows * depth + depth * part + rows * part),
            transcendentals=0,
        ),
        name="put_columns",
    )(*operands)


def body(teacher_hidden, teacher_head, student_hidden, student_head, kept):
    tokens = teacher_hidden.shape[0]
    features = student_hidden.shape[1]
    vocab_cols = teacher_head.shape[1]
    blocks_dev = vocab_cols // BLOCK
    row_blocks = tokens // BLOCK
    groups = lax.axis_size("seq")
    shards = lax.axis_size("vocab")
    seq_index = lax.axis_index("seq")
    vocab_index = lax.axis_index("vocab")
    piece_cols = vocab_cols // groups
    group_rows = tokens // groups

    def swap(value, k):
        return lax.ppermute(value, "seq", [(i, i ^ k) for i in range(groups)])

    pieces = [
        lax.dynamic_slice_in_dim(student_head, (seq_index ^ k) * piece_cols, piece_cols, 1)
        for k in range(groups)
    ]
    arrived = [pieces[0]] + [swap(pieces[k], k) for k in range(1, groups)]
    hidden_t = student_hidden.T

    share = tokens // shards
    rows = lax.dynamic_slice_in_dim(student_hidden, vocab_index * share, share, 0)
    rows = lax.all_gather(rows, "seq", axis=0)
    rows = lax.all_gather(rows, "vocab", axis=0)

    def hidden_of(peer):
        part = lax.dynamic_index_in_dim(rows, peer, 1, False)
        return part.reshape(tokens, features)

    first_block = vocab_index * blocks_dev
    kept_count = kept.shape[1]
    slots = min(blocks_dev, max(4, kept_count // shards))
    before = jnp.sum((kept < first_block).astype(jnp.int32), axis=1)
    slot_index = before[:, None] + jnp.arange(slots, dtype=jnp.int32)[None, :]
    slot_ids = jnp.take_along_axis(kept, jnp.minimum(slot_index, kept_count - 1), axis=1)
    local_ids = slot_ids - first_block
    slot_valid = (slot_index < kept_count) & (local_ids >= 0) & (local_ids < blocks_dev)
    safe_ids = jnp.clip(local_ids, 0, blocks_dev - 1)
    kernel_ids, hidden_t, *_ = lax.optimization_barrier((safe_ids, hidden_t, *pieces[1:]))
    partial_value = kept_partials(kernel_ids, teacher_hidden, teacher_head)
    compact = lax.psum(partial_value, "seq").reshape(row_blocks, BLOCK, slots, BLOCK)
    valid = slot_valid[:, None, :, None]
    local_top = jnp.max(jnp.where(valid, compact, masked_value), axis=(2, 3))
    weights = jnp.where(valid, jnp.exp(compact - local_top[:, :, None, None]), 0.0)
    local_stats = jnp.stack(
        [local_top, jnp.sum(weights, axis=(2, 3)), jnp.sum(weights * compact, axis=(2, 3))]
    ).reshape(3, tokens)
    all_stats = lax.all_gather(local_stats, "vocab")
    teacher_max = jnp.max(all_stats[:, 0], axis=0)
    scale = jnp.exp(all_stats[:, 0] - teacher_max)
    teacher_total = jnp.sum(all_stats[:, 1] * scale, axis=0)
    self_total = jnp.sum(all_stats[:, 2] * scale, axis=0)
    top_rows = teacher_max.reshape(row_blocks, BLOCK, 1, 1)
    total_rows = teacher_total.reshape(row_blocks, BLOCK, 1, 1)
    compact_prob = jnp.where(valid, jnp.exp(compact - top_rows), 0.0) / total_rows
    aligned = piece_cols % BLOCK == 0
    my_blocks = piece_cols // BLOCK if aligned else blocks_dev
    my_first = seq_index * my_blocks if aligned else 0
    column_ids = my_first + jnp.arange(my_blocks, dtype=jnp.int32)
    placer = (
        (safe_ids[:, :, None] == column_ids[None, None, :]) & slot_valid[:, :, None]
    ).astype(jnp.float32)
    teacher_prob = jnp.einsum(
        "rtmc,rmb->rtbc", compact_prob, placer, precision=lax.Precision.HIGHEST
    ).reshape(tokens, my_blocks * BLOCK)
    if not aligned:
        teacher_prob = lax.dynamic_slice_in_dim(
            teacher_prob, seq_index * piece_cols, piece_cols, 1
        )

    student_logits = None
    for k in range(groups):
        term = jnp.dot(
            hidden_of(seq_index ^ k), arrived[k], preferred_element_type=jnp.float32
        )
        student_logits = term if student_logits is None else student_logits + term
    student_top = jnp.max(student_logits, axis=1)
    student_local = jnp.sum(jnp.exp(student_logits - student_top[:, None]), axis=1)
    cross_local = jnp.sum(teacher_prob * student_logits, axis=1)
    stats = jnp.stack([student_top, student_local, cross_local])
    for axis in ("seq", "vocab"):
        gathered = lax.all_gather(stats, axis)
        top = jnp.max(gathered[:, 0], axis=0)
        stats = jnp.stack(
            [
                top,
                jnp.sum(gathered[:, 1] * jnp.exp(gathered[:, 0] - top), axis=0),
                jnp.sum(gathered[:, 2], axis=0),
            ]
        )
    student_max, student_total, cross_mean = stats[0], stats[1], stats[2]
    loss_all = (self_total / teacher_total - teacher_max - jnp.log(teacher_total)) - (
        cross_mean - student_max - jnp.log(student_total)
    )
    loss_rows = lax.dynamic_slice_in_dim(loss_all, seq_index * group_rows, group_rows, 0)
    student_prob = jnp.exp(student_logits - student_max[:, None]) / student_total[:, None]
    grad = (loss_scale * (student_prob - teacher_prob)).astype(jnp.bfloat16)

    if groups == 4:
        half = tokens // 2
        one, two = swap(grad, 1), swap(grad, 2)
        low = swap(two[:half], 1)
        high = swap(one[half:], 2)
        three = jnp.concatenate([low, high], axis=0)
        grads = [grad, one, two, three]
    else:
        grads = [grad] + [swap(grad, k) for k in range(1, groups)]
    hidden_total = None
    for k in range(groups):
        term = lax.dot_general(
            grads[k], pieces[k], (((1,), (1,)), ((), ())), preferred_element_type=jnp.float32
        )
        hidden_total = term if hidden_total is None else hidden_total + term
    hidden_grad = lax.psum_scatter(
        hidden_total, "vocab", scatter_dimension=0, tiled=True
    ).astype(jnp.bfloat16)
    if in_place(piece_cols):
        head_grad = None
        for k in range(groups):
            head_grad = put_columns(
                hidden_t, grads[k], head_grad, vocab_cols, seq_index ^ k
            )
        return (loss_rows, hidden_grad, head_grad)
    head_grad = jnp.zeros((features, vocab_cols), jnp.bfloat16)
    for k in range(groups):
        part = lax.dot_general(
            student_hidden, grads[k], (((0,), (0,)), ((), ())), preferred_element_type=jnp.float32
        ).astype(jnp.bfloat16)
        head_grad = lax.dynamic_update_slice_in_dim(
            head_grad, part, (seq_index ^ k) * piece_cols, 1
        )
    return (loss_rows, hidden_grad, head_grad)


def in_place(piece_cols):
    return piece_cols % TILE == 0


def solution(mesh):
    in_specs = (P(None, "seq"), P("seq", "vocab"), P(None, "seq"), P("seq", "vocab"), P())
    out_specs = (P("seq"), P("vocab", "seq"), P("seq", "vocab"))

    return jax.shard_map(body, mesh=mesh, in_specs=in_specs, out_specs=out_specs, check_vma=False)
```

profile of v0, /device:TPU:0, one launch (start us, length us, event | category | flops | bytes accessed | tf_op | source)
XLA Modules:
  0.0 697.7 jit_solution(5085973026515050044)
XLA Ops:
  8.1 0.9 convert_reduce_fusion
  9.2 1.5 gather_fusion
  10.8 0.7 broadcast_clamp_fusion.ids_ref
  11.5 2.5 copy.24
  14.0 9.8 %constant_dynamic-slice_fusion.7 = (bf16[896,2560]{1,0:T(8,128)(2,1)}, bf16[896,2560]{1,0:T(8,128)(2,1)}, bf16[896,2560]{1,0:T(8,128)(2,1)}) fusion(bf16[896,10240]{1,0:T(8,128)(2,1)} %param.8, s32[]{:T(128)S(6)} %select_n.87, s32[]{:T(128)S(6)} %select_n.88, s32[]{:T(128)S(6)} %select_n.89), kind=kLoop, calls=%fused_computation.81 | loop fusion | bytes 27525132 | tf_op jit(solution)/shard_map/dynamic_slice | solution.py:105
  23.8 48.2 %kept_partials.1 = f32[1024,1024]{1,0:T(8,128)} custom-call(s32[8,8]{1,0:T(8,128)} %broadcast_clamp_fusion.ids_ref, bf16[1024,2048]{1,0:T(8,128)(2,1)} %hidden_ref.1, bf16[2048,10240]{1,0:T(8,128)(2,1)} %head_ref.1), custom_call_target="tpu_custom_call" | custom-call | flops 4294967296 | bytes 33554432 | tf_op jit(solution)/shard_map/kept_partials/pallas_call | solution.py:24
  72.1 21.1 %all-gather = bf16[512,896]{1,0:T(8,128)(2,1)} all-gather(bf16[128,896]{1,0:T(8,128)(2,1)S(1)} %constant_dynamic-slice_fusion.4), channel_id=2, replica_groups=mesh['seq'=4,'vocab'=8] {'seq'}, dimensions={0}, use_global_device_ids=true | all-gather | bytes 1146880 | tf_op jit(solution)/shard_map/all_gather | solution.py:113
  93.2 1.0 collective-permute-start.1
  94.3 1.1 collective-permute-start
  95.3 1.5 collective-permute-start.2
  96.9 145.8 %all-reduce.2.cloned.1.call-done = f32[1024,1024]{1,0:T(8,128)} async-done(((f32[1024,1024]{1,0:T(8,128)}), f32[1024,1024]{1,0:T(8,128)}) %all-reduce.2.cloned.1.call-update) | async-done | bytes 4194320 | tf_op jit(solution)/shard_map/psum | solution.py:131
  242.7 3.4 copy.44
  246.1 0.3 broadcast_in_dim.42
  246.4 0.7 select_reduce_fusion
  247.1 2.0 fusion.8
  249.1 14.1 %all_gather.27 = f32[8,3,1024]{2,1,0:T(4,128)S(1)} all-gather(f32[1,3,1024]{2,1,0:T(4,128)S(1)} %pad_maximum_fusion), channel_id=1, replica_groups=mesh['seq'=4,'vocab'=8] {'vocab'}, dimensions={0}, use_global_device_ids=true | all-gather | bytes 110592 | tf_op jit(solution)/shard_map/all_gather | solution.py:138
  263.3 9.6 %fusion.6 = f32[8,20,128,128]{3,1,2,0:T(8,128)} fusion(f32[8,128]{1,0:T(8,128)S(1)} %bitcast.147, f32[8,128]{1,0:T(8,128)S(1)} %bitcast.146, pred[8,8]{1,0:T(8,128)(4,1)S(1)} %fusion.43, s32[20]{0:T(128)S(1)} %iota_add_fusion.1, s32[8,8]{1,0:T(8,128)S(1)} %copy-done.7, f32[8,128,8,128]{3,2,1,0:T(8,128)S(1)} %bitcast.131), kind=kOutput, calls=%fused_computation.12 | convolution fusion | flops 254806528 | bytes 14688656 | tf_op jit(solution)/shard_map/rtmc,rmb->rtbc/dot_general | solution.py:153
  272.9 3.9 constant_dynamic-slice_fusion.2
  276.8 10.4 %fusion.51 = f32[1024,2560]{1,0:T(8,128)} fusion(bf16[1024,896]{1,0:T(8,128)(2,1)S(1)} %bitcast.145, bf16[896,2560]{1,0:T(8,128)(2,1)} %collective-permute-done.1), kind=kOutput, calls=%fused_computation.92 | convolution fusion | flops 4697620480 | bytes 16908288 | tf_op jit(solution)/shard_map/dot_general | solution.py:163
  287.2 10.5 %fusion.50 = f32[1024,2560]{1,0:T(8,128)} fusion(bf16[1024,896]{1,0:T(8,128)(2,1)S(1)} %bitcast.144, bf16[896,2560]{1,0:T(8,128)(2,1)} %collective-permute-done), kind=kOutput, calls=%fused_computation.91 | convolution fusion | flops 4697620480 | bytes 16908288 | tf_op jit(solution)/shard_map/dot_general | solution.py:163
  297.7 10.5 %fusion.11 = f32[1024,2560]{1,0:T(8,128)} fusion(bf16[1024,896]{1,0:T(8,128)(2,1)S(1)} %bitcast.143, bf16[896,10240]{1,0:T(8,128)(2,1)} %param.8, s32[]{:T(128)S(6)} %select_n.94), kind=kOutput, calls=%fused_computation.19 | convolution fusion | flops 4697620480 | bytes 16908292 | tf_op jit(solution)/shard_map/dot_general | solution.py:163
  308.3 43.3 %collective-permute-done.2 = bf16[896,2560]{1,0:T(8,128)(2,1)} collective-permute-done((bf16[896,2560]{1,0:T(8,128)(2,1)}, bf16[896,2560]{1,0:T(8,128)(2,1)}, u32[]{:S(2)}, u32[]{:S(2)}) %collective-permute-start.2) | collective-permute-done | bytes 4587552 | tf_op jit(solution)/shard_map/ppermute | solution.py:102
  351.6 17.1 %fusion.47 = (f32[1024]{0:T(1024)S(1)}, f32[1024,2560]{1,0:T(8,128)}) fusion(f32[1024,2560]{1,0:T(8,128)} %fusion.51, f32[1024,2560]{1,0:T(8,128)} %fusion.11, f32[1024,2560]{1,0:T(8,128)} %fusion.50, bf16[1024,896]{1,0:T(8,128)(2,1)S(1)} %bitcast.135, bf16[896,2560]{1,0:T(8,128)(2,1)} %collective-permute-done.2), kind=kOutput, calls=%fused_computation.88 | convolution fusion | flops 4708105216 | bytes 48369664 | tf_op jit(solution)/shard_map/dot_general | solution.py:163
  368.7 20.0 %exponential_reduce_fusion = (f32[1024]{0:T(1024)S(1)}, f32[1024]{0:T(1024)S(1)}) fusion(f32[1024,2560]{1,0:T(8,128)} %get-tuple-element.18, f32[1024]{0:T(1024)S(1)} %get-tuple-element.17, f32[128,8,20,128]{3,2,1,0:T(8,128)} %bitcast.122), kind=kLoop, calls=%fused_computation.6 | loop fusion | flops 10483712 | bytes 20983808 | tf_op jit(solution)/shard_map/reduce_sum | solution.py:168
  388.8 37.8 %all-gather.4 = f32[4,3,1024]{2,1,0:T(4,128)S(1)} all-gather(f32[1,3,1024]{2,1,0:T(4,128)S(1)} %maximum_bitcast_fusion), channel_id=4, replica_groups=mesh['seq'=4,'vocab'=8] {'seq'}, dimensions={0}, use_global_device_ids=true | all-gather | bytes 61440 | tf_op jit(solution)/shard_map/all_gather | solution.py:172
  426.7 14.0 %all-gather.5 = f32[8,3,1024]{2,1,0:T(4,128)S(1)} all-gather(f32[1,3,1024]{2,1,0:T(4,128)S(1)} %maximum_bitcast_fusion.1), channel_id=5, replica_groups=mesh['seq'=4,'vocab'=8] {'vocab'}, dimensions={0}, use_global_device_ids=true | all-gather | bytes 110592 | tf_op jit(solution)/shard_map/all_gather | solution.py:172
  440.9 4.8 fusion.1.right_ref
  445.7 2.1 collective-permute-start.4
  447.9 113.5 %collective-permute-done.4.right_ref = bf16[1024,2560]{1,0:T(8,128)(2,1)S(1)} collective-permute-done((bf16[1024,2560]{1,0:T(8,128)(2,1)S(1)}, bf16[1024,2560]{1,0:T(8,128)(2,1)S(1)}, u32[]{:S(2)}, u32[]{:S(2)}) %collective-permute-start.4) | collective-permute-done | bytes 5242912 | tf_op jit(solution)/shard_map/ppermute | solution.py:102
  561.4 1.8 slice.58
  563.1 1.7 collective-permute-start.5
  564.9 10.4 %fusion.9 = f32[1024,896]{1,0:T(8,128)} fusion(bf16[1024,2560]{1,0:T(8,128)(2,1)S(1)} %fusion.1.right_ref, bf16[896,10240]{1,0:T(8,128)(2,1)} %param.8, s32[]{:T(128)S(6)} %select_n.94), kind=kOutput, calls=%fused_computation.17 | convolution fusion | flops 4697620480 | bytes 13500420 | tf_op jit(solution)/shard_map/dot_general | solution.py:200
  575.2 0.2 slice.59
  575.4 1.8 collective-permute-start.6
  577.3 7.4 %fusion.53 = f32[1024,896]{1,0:T(8,128)} fusion(bf16[1024,2560]{1,0:T(8,128)(2,1)S(1)} %collective-permute-done.4.right_ref, bf16[896,2560]{1,0:T(8,128)(2,1)S(1)} %bitcast.141), kind=kOutput, calls=%fused_computation.94 | convolution fusion | flops 4697620480 | bytes 13500416 | tf_op jit(solution)/shard_map/dot_general | solution.py:200
  584.7 7.5 %fusion.52 = f32[1024,896]{1,0:T(8,128)} fusion(bf16[1024,2560]{1,0:T(8,128)(2,1)S(1)} %collective-permute-done.3.right_ref, bf16[896,2560]{1,0:T(8,128)(2,1)S(1)} %bitcast.139), kind=kOutput, calls=%fused_computation.93 | convolution fusion | flops 4697620480 | bytes 13500416 | tf_op jit(solution)/shard_map/dot_general | solution.py:200
  592.2 29.7 %collective-permute-done.5 = bf16[512,2560]{1,0:T(8,128)(2,1)} collective-permute-done((bf16[512,2560]{1,0:T(8,128)(2,1)}, bf16[512,2560]{1,0:T(8,128)(2,1)}, u32[]{:S(2)}, u32[]{:S(2)}) %collective-permute-start.5) | collective-permute-done | bytes 2621472 | tf_op jit(solution)/shard_map/ppermute | solution.py:102
  622.0 1.9 constant_dynamic-update-slice_fusion.1
  623.9 10.1 %collective-permute-done.6 = bf16[512,2560]{1,0:T(8,128)(2,1)S(1)} collective-permute-done((bf16[512,2560]{1,0:T(8,128)(2,1)S(1)}, bf16[512,2560]{1,0:T(8,128)(2,1)S(1)}, u32[]{:S(2)}, u32[]{:S(2)}) %collective-permute-start.6) | collective-permute-done | bytes 2621472 | tf_op jit(solution)/shard_map/ppermute | solution.py:102
  634.2 2.2 copy-done.5
  636.5 9.6 %add_add_fusion.1 = f32[1024,896]{1,0:T(8,128)} fusion(f32[1024,896]{1,0:T(8,128)} %fusion.53, f32[1024,896]{1,0:T(8,128)S(1)} %copy-done.8, f32[1024,896]{1,0:T(8,128)} %fusion.52, bf16[1024,2560]{1,0:T(8,128)(2,1)S(1)} %constant_dynamic-update-slice_fusion.right_ref, bf16[896,2560]{1,0:T(8,128)(2,1)S(1)} %bitcast.137), kind=kOutput, calls=%fused_computation.21 | convolution fusion | flops 4700372992 | bytes 24510464 | tf_op jit(solution)/shard_map/dot_general | solution.py:200
  646.1 0.6 dynamic_slice.40
  646.7 9.2 %put_columns.4.rest_0_ = bf16[896,10240]{1,0:T(8,128)(2,1)} custom-call(s32[1]{0:T(128)} %bitcast.30.offset_ref, bf16[896,1024]{1,0:T(8,128)(2,1)} %bitcast.126, bf16[1024,2560]{1,0:T(8,128)(2,1)} %copy-done.2), custom_call_target="tpu_custom_call" | custom-call | flops 4697620480 | bytes 11665408 | tf_op jit(solution)/shard_map/put_columns/pallas_call | solution.py:69
  656.0 9.3 %put_columns.5.rest_0_ = bf16[896,10240]{1,0:T(8,128)(2,1)} custom-call(s32[1]{0:T(128)} %bitcast.29.offset_ref, bf16[896,1024]{1,0:T(8,128)(2,1)} %bitcast.127, bf16[1024,2560]{1,0:T(8,128)(2,1)} %copy-done.4, bf16[896,10240]{1,0:T(8,128)(2,1)} %put_columns.4.rest_0_), custom_call_target="tpu_custom_call", output_to_operand_aliasing={{}: (3, {})} | custom-call | flops 4697620480 | bytes 11665408 | tf_op jit(solution)/shard_map/put_columns/pallas_call | solution.py:69
  665.3 9.3 %put_columns.6.rest_0_ = bf16[896,10240]{1,0:T(8,128)(2,1)} custom-call(s32[1]{0:T(128)} %bitcast.28.offset_ref, bf16[896,1024]{1,0:T(8,128)(2,1)} %bitcast.128, bf16[1024,2560]{1,0:T(8,128)(2,1)} %copy-done.3, bf16[896,10240]{1,0:T(8,128)(2,1)} %put_columns.5.rest_0_), custom_call_target="tpu_custom_call", output_to_operand_aliasing={{}: (3, {})} | custom-call | flops 4697620480 | bytes 11665408 | tf_op jit(solution)/shard_map/put_columns/pallas_call | solution.py:69
  674.6 9.3 %put_columns.7 = bf16[896,10240]{1,0:T(8,128)(2,1)} custom-call(s32[1]{0:T(128)} %bitcast.27.offset_ref, bf16[896,1024]{1,0:T(8,128)(2,1)} %bitcast.129, bf16[1024,2560]{1,0:T(8,128)(2,1)} %copy-done.5, bf16[896,10240]{1,0:T(8,128)(2,1)} %put_columns.6.rest_0_), custom_call_target="tpu_custom_call", output_to_operand_aliasing={{}: (3, {})} | custom-call | flops 4697620480 | bytes 11665408 | tf_op jit(solution)/shard_map/put_columns/pallas_call | solution.py:69
  683.9 4.4 reduce-scatter.2.cloned.1.call-done
  688.3 1.7 convert_element_type.12
  (67 shorter events, 1.3 us)
Async XLA Ops:
  8.0 3.5 copy-start.6
  8.0 234.7 %all-reduce.2.cloned.1.call-start = ((), (), s32[]{:S(2)}) async-start(), calls=%async_computation.1 | async-start | bytes 8388608 | tf_op jit(solution)/shard_map/psum | solution.py:131
  72.0 200.9 %all-gather.8.cloned.1.call-start = ((), (), s32[]{:S(2)}) async-start(), calls=%async_computation.3 | async-start | bytes 8257536 | tf_op jit(solution)/shard_map/all_gather | solution.py:114
  93.2 595.1 %reduce-scatter.2.cloned.1.call-start = ((), (), s32[]{:S(2)}) async-start(), calls=%async_computation.2 | async-start | bytes 4128768 | tf_op jit(solution)/shard_map/reduce_scatter | solution.py:204
  93.2 183.6 %collective-permute-start.1 = (bf16[896,2560]{1,0:T(8,128)(2,1)}, bf16[896,2560]{1,0:T(8,128)(2,1)}, u32[]{:S(2)}, u32[]{:S(2)}) collective-permute-start(bf16[896,2560]{1,0:T(8,128)(2,1)} %get-tuple-element.20), channel_id=1, source_target_pairs={{0,16},{8,24},{16,0},{24,8},{1,17},{9,25},{17,1},{25,9},{2,18},{10... | collective-permute-start | bytes 13762568 | tf_op jit(solution)/shard_map/ppermute | solution.py:102
  94.3 193.0 %collective-permute-start = (bf16[896,2560]{1,0:T(8,128)(2,1)}, bf16[896,2560]{1,0:T(8,128)(2,1)}, u32[]{:S(2)}, u32[]{:S(2)}) collective-permute-start(bf16[896,2560]{1,0:T(8,128)(2,1)} %get-tuple-element.19), channel_id=1, source_target_pairs={{0,8},{8,0},{16,24},{24,16},{1,9},{9,1},{17,25},{25,17},{2,10},{10... | collective-permute-start | bytes 13762568 | tf_op jit(solution)/shard_map/ppermute | solution.py:102
  95.3 256.3 %collective-permute-start.2 = (bf16[896,2560]{1,0:T(8,128)(2,1)}, bf16[896,2560]{1,0:T(8,128)(2,1)}, u32[]{:S(2)}, u32[]{:S(2)}) collective-permute-start(bf16[896,2560]{1,0:T(8,128)(2,1)} %get-tuple-element.21), channel_id=1, source_target_pairs={{0,24},{8,16},{16,8},{24,0},{1,25},{9,17},{17,9},{25,1},{2,26},{10... | collective-permute-start | bytes 13762568 | tf_op jit(solution)/shard_map/ppermute | solution.py:102
  242.7 3.7 copy-start.1
  246.4 16.9 %copy-start.7 = (s32[8,8]{1,0:T(8,128)S(1)}, s32[8,8]{1,0:T(8,128)}, u32[]{:S(2)}) copy-start(s32[8,8]{1,0:T(8,128)} %broadcast_clamp_fusion.ids_ref) | copy-start | bytes 772
  368.7 72.2 %slice-start = ((s8[12582912]{0:T(1024)(128)(4,1)}), s8[4194304]{0:T(1024)(128)(4,1)S(1)}, s32[]{:S(2)}) async-start(s8[12582912]{0:T(1024)(128)(4,1)} %bitcast.123), calls=%async_computation.4 | async-start | bytes 8388608
  368.7 72.2 %slice-start.1 = ((s8[12582912]{0:T(1024)(128)(4,1)}), s8[4194304]{0:T(1024)(128)(4,1)S(1)}, s32[]{:S(2)}) async-start(s8[12582912]{0:T(1024)(128)(4,1)} %bitcast.123), calls=%async_computation.5 | async-start | bytes 8388608
  368.7 72.2 %slice-start.2 = ((s8[12582912]{0:T(1024)(128)(4,1)}), s8[4194304]{0:T(1024)(128)(4,1)S(1)}, s32[]{:S(2)}) async-start(s8[12582912]{0:T(1024)(128)(4,1)} %bitcast.123), calls=%async_computation.6 | async-start | bytes 8388608
  368.7 72.2 %copy-start = (f32[1024,2560]{1,0:T(8,128)S(1)}, f32[1024,2560]{1,0:T(8,128)}, u32[]{:S(2)}) copy-start(f32[1024,2560]{1,0:T(8,128)} %get-tuple-element.18) | copy-start | bytes 31457284
  445.7 129.5 %copy-start.2 = (bf16[1024,2560]{1,0:T(8,128)(2,1)}, bf16[1024,2560]{1,0:T(8,128)(2,1)S(1)}, u32[]{:S(2)}) copy-start(bf16[1024,2560]{1,0:T(8,128)(2,1)S(1)} %fusion.1.right_ref) | copy-start | bytes 15728644
  445.7 115.6 %collective-permute-start.4 = (bf16[1024,2560]{1,0:T(8,128)(2,1)S(1)}, bf16[1024,2560]{1,0:T(8,128)(2,1)S(1)}, u32[]{:S(2)}, u32[]{:S(2)}) collective-permute-start(bf16[1024,2560]{1,0:T(8,128)(2,1)S(1)} %fusion.1.right_ref), channel_id=1, source_target_pairs={{0,16},{8,24},{16,0},{24,8},{1,17},{9,25},{17,1},{25,9},{2,18},{10... | collective-permute-start | bytes 15728648 | tf_op jit(solution)/shard_map/ppermute | solution.py:102
  447.8 127.4 %collective-permute-start.3 = (bf16[1024,2560]{1,0:T(8,128)(2,1)S(1)}, bf16[1024,2560]{1,0:T(8,128)(2,1)S(1)}, u32[]{:S(2)}, u32[]{:S(2)}) collective-permute-start(bf16[1024,2560]{1,0:T(8,128)(2,1)S(1)} %fusion.1.right_ref), channel_id=1, source_target_pairs={{0,8},{8,0},{16,24},{24,16},{1,9},{9,1},{17,25},{25,17},{2,10},{10... | collective-permute-start | bytes 15728648 | tf_op jit(solution)/shard_map/ppermute | solution.py:102
  561.4 15.9 %copy-start.3 = (bf16[1024,2560]{1,0:T(8,128)(2,1)}, bf16[1024,2560]{1,0:T(8,128)(2,1)S(1)}, u32[]{:S(2)}) copy-start(bf16[1024,2560]{1,0:T(8,128)(2,1)S(1)} %collective-permute-done.4.right_ref) | copy-start | bytes 15728644
  561.4 15.9 %slice-start.7 = ((s8[4587520]{0:T(1024)(128)(4,1)}), s8[4194304]{0:T(1024)(128)(4,1)S(1)}, s32[]{:S(2)}) async-start(s8[4587520]{0:T(1024)(128)(4,1)} %bitcast.140), calls=%async_computation.11 | async-start | bytes 8388608
  563.1 14.1 %slice-start.8 = ((s8[4587520]{0:T(1024)(128)(4,1)}), s8[393216]{0:T(1024)(128)(4,1)S(1)}, s32[]{:S(2)}) async-start(s8[4587520]{0:T(1024)(128)(4,1)} %bitcast.140), calls=%async_computation.12 | async-start | bytes 786432
  563.1 58.9 %collective-permute-start.5 = (bf16[512,2560]{1,0:T(8,128)(2,1)}, bf16[512,2560]{1,0:T(8,128)(2,1)}, u32[]{:S(2)}, u32[]{:S(2)}) collective-permute-start(bf16[512,2560]{1,0:T(8,128)(2,1)} %slice.58), channel_id=1, source_target_pairs={{0,8},{8,0},{16,24},{24,16},{1,9},{9,1},{17,25},{25,17},{2,10},{10... | collective-permute-start | bytes 7864328 | tf_op jit(solution)/shard_map/ppermute | solution.py:102
  575.2 9.5 %copy-start.4 = (bf16[1024,2560]{1,0:T(8,128)(2,1)}, bf16[1024,2560]{1,0:T(8,128)(2,1)S(1)}, u32[]{:S(2)}) copy-start(bf16[1024,2560]{1,0:T(8,128)(2,1)S(1)} %collective-permute-done.3.right_ref) | copy-start | bytes 15728644
  575.2 9.5 %slice-start.5 = ((s8[4587520]{0:T(1024)(128)(4,1)}), s8[4194304]{0:T(1024)(128)(4,1)S(1)}, s32[]{:S(2)}) async-start(s8[4587520]{0:T(1024)(128)(4,1)} %bitcast.138), calls=%async_computation.9 | async-start | bytes 8388608
  575.4 9.3 %slice-start.6 = ((s8[4587520]{0:T(1024)(128)(4,1)}), s8[393216]{0:T(1024)(128)(4,1)S(1)}, s32[]{:S(2)}) async-start(s8[4587520]{0:T(1024)(128)(4,1)} %bitcast.138), calls=%async_computation.10 | async-start | bytes 786432
  575.4 58.6 %collective-permute-start.6 = (bf16[512,2560]{1,0:T(8,128)(2,1)S(1)}, bf16[512,2560]{1,0:T(8,128)(2,1)S(1)}, u32[]{:S(2)}, u32[]{:S(2)}) collective-permute-start(bf16[512,2560]{1,0:T(8,128)(2,1)S(1)} %slice.59), channel_id=1, source_target_pairs={{0,16},{8,24},{16,0},{24,8},{1,17},{9,25},{17,1},{25,9},{2,18},{10... | collective-permute-start | bytes 7864328 | tf_op jit(solution)/shard_map/ppermute | solution.py:102
  577.3 59.2 %slice-start.3 = ((s8[4587520]{0:T(1024)(128)(4,1)}), s8[4194304]{0:T(1024)(128)(4,1)S(1)}, s32[]{:S(2)}) async-start(s8[4587520]{0:T(1024)(128)(4,1)} %bitcast.136), calls=%async_computation.7 | async-start | bytes 8388608
  584.7 51.7 %slice-start.4 = ((s8[4587520]{0:T(1024)(128)(4,1)}), s8[393216]{0:T(1024)(128)(4,1)S(1)}, s32[]{:S(2)}) async-start(s8[4587520]{0:T(1024)(128)(4,1)} %bitcast.136), calls=%async_computation.8 | async-start | bytes 786432
  592.2 44.2 %copy-start.8 = (f32[1024,896]{1,0:T(8,128)S(1)}, f32[1024,896]{1,0:T(8,128)}, u32[]{:S(2)}) copy-start(f32[1024,896]{1,0:T(8,128)} %fusion.9) | copy-start | bytes 11010052
  634.2 2.2 copy-start.5
Sparse Core Ops, SparseCore 0:
  72.1 170.5 all-reduce.1
Sparse Core Ops, SparseCore 1:
  93.3 73.5 all-gather.7
  646.1 42.1 reduce-scatter.1
where the time goes:
time: 705 us; the launch traced here: 698 us
  waiting for transfers between devices  347 us (49%)
  matrix products  93 us (13%)
  blocking collectives  87 us (12%)
  Pallas kernels  85.3 us (12%)
  other arithmetic  31.4 us (4%)
  local copies, waits for them, and re-layouts  28.6 us (4%)
  between operations  16 us (2%)
  starting transfers between devices  9.4 us (1%)
    ppermute x7, waiting for transfers between devices, swap(): return lax.ppermute(value, 'seq', [(i, i ^ k) for i in range(groups)])  197 us
    psum x1, waiting for transfers between devices, body(): lax.psum(partial_value, 'seq').reshape(row_blocks, BLOCK, slots, BLOCK)  146 us
    all_gather x2, blocking collectives, body(): gathered = lax.all_gather(stats, axis)  51.8 us
    dot_general x4, matrix products, body(): jnp.dot(hidden_of(seq_index ^ k), arrived[k], preferred_element_type=jnp....  48.5 us
    pallas_call x1, Pallas kernels, kept_partials(): pl.pallas_call(kept_kernel, out_shape=jax.ShapeDtypeStruct((row_blocks *...  48.2 us
    pallas_call x4, Pallas kernels, put_columns(): pl.pallas_call(columns_kernel, out_shape=jax.ShapeDtypeStruct((rows, cols...  37.1 us
    dot_general x4, matrix products, body(): lax.dot_general(grads[k], pieces[k], (((1,), (1,)), ((), ())), preferred_...  34.9 us
    all_gather x1, blocking collectives, body(): rows = lax.all_gather(rows, 'seq', axis=0)  21.1 us
  transfers between devices with their start and end apart: 10, of which 6 were waited for; matrix products, arithmetic and copies ran while one was open for 12% of the time, Pallas kernels for 5%

commit v1 on v0

--- a/solution.py
+++ b/solution.py
@@ -110,12 +110,11 @@
 
     share = tokens // shards
     rows = lax.dynamic_slice_in_dim(student_hidden, vocab_index * share, share, 0)
-    rows = lax.all_gather(rows, "seq", axis=0)
+    rows = jnp.stack([rows] + [swap(rows, k) for k in range(1, groups)])
     rows = lax.all_gather(rows, "vocab", axis=0)
 
-    def hidden_of(peer):
-        part = lax.dynamic_index_in_dim(rows, peer, 1, False)
-        return part.reshape(tokens, features)
+    def hidden_of(k):
+        return rows[:, k].reshape(tokens, features)
 
     first_block = vocab_index * blocks_dev
     kept_count = kept.shape[1]
@@ -128,7 +127,23 @@
     safe_ids = jnp.clip(local_ids, 0, blocks_dev - 1)
     kernel_ids, hidden_t, *_ = lax.optimization_barrier((safe_ids, hidden_t, *pieces[1:]))
     partial_value = kept_partials(kernel_ids, teacher_hidden, teacher_head)
-    compact = lax.psum(partial_value, "seq").reshape(row_blocks, BLOCK, slots, BLOCK)
+    student_logits = None
+    for k in range(groups):
+        term = jnp.dot(
+            hidden_of(k), arrived[k], preferred_element_type=jnp.float32
+        )
+        student_logits = term if student_logits is None else student_logits + term
+    student_top = jnp.max(student_logits, axis=1)
+    student_local = jnp.sum(jnp.exp(student_logits - student_top[:, None]), axis=1)
+    stats = jnp.stack([student_top, student_local])
+    for axis in ("seq", "vocab"):
+        gathered = lax.all_gather(stats, axis)
+        top = jnp.max(gathered[:, 0], axis=0)
+        total = jnp.sum(gathered[:, 1] * jnp.exp(gathered[:, 0] - top), axis=0)
+        stats = jnp.stack([top, total])
+    compact, stats = lax.optimization_barrier((lax.psum(partial_value, "seq"), stats))
+    student_max, student_total = stats[0], stats[1]
+    compact = compact.reshape(row_blocks, BLOCK, slots, BLOCK)
     valid = slot_valid[:, None, :, None]
     local_top = jnp.max(jnp.where(valid, compact, masked_value), axis=(2, 3))
     weights = jnp.where(valid, jnp.exp(compact - local_top[:, :, None, None]), 0.0)
@@ -158,31 +173,7 @@
             teacher_prob, seq_index * piece_cols, piece_cols, 1
         )
 
-    student_logits = None
-    for k in range(groups):
-        term = jnp.dot(
-            hidden_of(seq_index ^ k), arrived[k], preferred_element_type=jnp.float32
-        )
-        student_logits = term if student_logits is None else student_logits + term
-    student_top = jnp.max(student_logits, axis=1)
-    student_local = jnp.sum(jnp.exp(student_logits - student_top[:, None]), axis=1)
     cross_local = jnp.sum(teacher_prob * student_logits, axis=1)
-    stats = jnp.stack([student_top, student_local, cross_local])
-    for axis in ("seq", "vocab"):
-        gathered = lax.all_gather(stats, axis)
-        top = jnp.max(gathered[:, 0], axis=0)
-        stats = jnp.stack(
-            [
-                top,
-                jnp.sum(gathered[:, 1] * jnp.exp(gathered[:, 0] - top), axis=0),
-                jnp.sum(gathered[:, 2], axis=0),
-            ]
-        )
-    student_max, student_total, cross_mean = stats[0], stats[1], stats[2]
-    loss_all = (self_total / teacher_total - teacher_max - jnp.log(teacher_total)) - (
-        cross_mean - student_max - jnp.log(student_total)
-    )
-    loss_rows = lax.dynamic_slice_in_dim(loss_all, seq_index * group_rows, group_rows, 0)
     student_prob = jnp.exp(student_logits - student_max[:, None]) / student_total[:, None]
     grad = (loss_scale * (student_prob - teacher_prob)).astype(jnp.bfloat16)
 
@@ -201,9 +192,17 @@
             grads[k], pieces[k], (((1,), (1,)), ((), ())), preferred_element_type=jnp.float32
         )
         hidden_total = term if hidden_total is None else hidden_total + term
+    hidden_total, cross_local = lax.optimization_barrier((hidden_total, cross_local))
     hidden_grad = lax.psum_scatter(
         hidden_total, "vocab", scatter_dimension=0, tiled=True
     ).astype(jnp.bfloat16)
+    cross_mean = cross_local
+    for axis in ("seq", "vocab"):
+        cross_mean = jnp.sum(lax.all_gather(cross_mean, axis), axis=0)
+    loss_all = (self_total / teacher_total - teacher_max - jnp.log(teacher_total)) - (
+        cross_mean - student_max - jnp.log(student_total)
+    )
+    loss_rows = lax.dynamic_slice_in_dim(loss_all, seq_index * group_rows, group_rows, 0)
     if in_place(piece_cols):
         head_grad = None
         for k in range(groups):

time: 705 us -> 631 us (0.90)
  waiting for transfers between devices: 347 us -> 313 us
  blocking collectives: 87 us -> 58.4 us
  other arithmetic: 31.4 us -> 19.2 us
    psum x1, waiting for transfers between devices: 146 us -> 0.03 us  [body(): lax.psum(partial_value, 'seq')]
    ppermute x7 -> x10, waiting for transfers between devices: 197 us -> 306 us  [swap(): return lax.ppermute(value, 'seq', [(i, i ^ k) for i in range(groups)])]
    all_gather x2, blocking collectives: 51.8 us -> 23.2 us  [body(): gathered = lax.all_gather(stats, axis)]
    reduce_sum x1, other arithmetic: 20 us -> 5.64 us  [body(): jnp.sum(jnp.exp(student_logits - student_top[:, None]), axis=1)]
    all_gather x1 -> x2, blocking collectives: 21.1 us -> 21.3 us  [body(): cross_mean = jnp.sum(lax.all_gather(cross_mean, axis), axis=0)]
  transfers between devices with their start and end apart: 10 -> 13, of which waited for: 6 -> 9; matrix products, arithmetic and copies ran while one was open for 12% -> 17% of each run, Pallas kernels for 5% -> 14%
where the time goes in v1:
time: 631 us; the launch traced here: 626 us
  waiting for transfers between devices  313 us (50%)
  matrix products  95.9 us (15%)
  Pallas kernels  85.6 us (14%)
  blocking collectives  58.4 us (9%)
  local copies, waits for them, and re-layouts  26 us (4%)
  other arithmetic  19.2 us (3%)
  between operations  16.1 us (3%)
  starting transfers between devices  11.7 us (2%)
    ppermute x10, waiting for transfers between devices, swap(): return lax.ppermute(value, 'seq', [(i, i ^ k) for i in range(groups)])  306 us
    dot_general x4, matrix products, body(): term = jnp.dot(hidden_of(k), arrived[k], preferred_element_type=jnp.float32)  49.7 us
    pallas_call x1, Pallas kernels, kept_partials(): pl.pallas_call(kept_kernel, out_shape=jax.ShapeDtypeStruct((row_blocks *...  48.5 us
    dot_general x4, matrix products, body(): lax.dot_general(grads[k], pieces[k], (((1,), (1,)), ((), ())), preferred_...  40 us
    pallas_call x4, Pallas kernels, put_columns(): pl.pallas_call(columns_kernel, out_shape=jax.ShapeDtypeStruct((rows, cols...  37.1 us
    all_gather x2, blocking collectives, body(): gathered = lax.all_gather(stats, axis)  23.2 us
    all_gather x2, blocking collectives, body(): cross_mean = jnp.sum(lax.all_gather(cross_mean, axis), axis=0)  21.3 us
    all_gather x1, blocking collectives, body(): all_stats = lax.all_gather(local_stats, 'vocab')  14 us
  transfers between devices with their start and end apart: 13, of which 9 were waited for; matrix products, arithmetic and copies ran while one was open for 17% of the time, Pallas kernels for 14%

profile of v1, /device:TPU:0, one launch (start us, length us, event | category | flops | bytes accessed | tf_op | source)
XLA Modules:
  0.0 625.8 jit_solution(11463020609627334553)
XLA Ops:
  8.0 1.0 constant_dynamic-slice_fusion
  9.0 4.0 collective-permute-start.2
  13.6 1.0 fusion.68
  14.6 4.9 collective-permute-done.2
  19.5 4.0 collective-permute-done.1
  23.8 1.1 pad_maximum_fusion
  25.0 10.3 %constant_dynamic-slice_fusion.1 = (bf16[896,2560]{1,0:T(8,128)(2,1)}, bf16[896,2560]{1,0:T(8,128)(2,1)}, bf16[896,2560]{1,0:T(8,128)(2,1)}) fusion(bf16[896,10240]{1,0:T(8,128)(2,1)} %param.8, s32[]{:T(128)S(6)} %select_n.76, s32[]{:T(128)S(6)} %select_n.75, s32[]{:T(128)S(6)} %select_n.74), kind=kLoop, calls=%fused_computation.76 | loop fusion | bytes 27525132 | tf_op jit(solution)/shard_map/dynamic_slice | solution.py:105
  35.3 1.3 collective-permute-start.4
  37.2 1.6 collective-permute-start.5
  39.0 0.7 gather_fusion
  39.9 0.7 broadcast_clamp_fusion.ids_ref
  40.5 2.5 copy.32
  43.1 48.5 %kept_partials.1 = f32[1024,1024]{1,0:T(8,128)} custom-call(s32[8,8]{1,0:T(8,128)} %broadcast_clamp_fusion.ids_ref, bf16[1024,2048]{1,0:T(8,128)(2,1)} %hidden_ref.1, bf16[2048,10240]{1,0:T(8,128)(2,1)} %head_ref.1), custom_call_target="tpu_custom_call" | custom-call | flops 4294967296 | bytes 33554432 | tf_op jit(solution)/shard_map/kept_partials/pallas_call | solution.py:24
  92.0 6.9 %all-gather.9.cloned.1.call-done = bf16[32,128,896]{2,1,0:T(8,128)(2,1)} async-done(((bf16[4,128,896]{2,1,0:T(8,128)(2,1)}), bf16[32,128,896]{2,1,0:T(8,128)(2,1)}) %all-gather.9.cloned.1.call-update) | async-done | bytes 7340048 | tf_op jit(solution)/shard_map/all_gather | solution.py:114
  98.9 3.9 fusion.47
  102.8 63.3 %collective-permute-done.4 = bf16[896,2560]{1,0:T(8,128)(2,1)} collective-permute-done((bf16[896,2560]{1,0:T(8,128)(2,1)}, bf16[896,2560]{1,0:T(8,128)(2,1)}, u32[]{:S(2)}, u32[]{:S(2)}) %collective-permute-start.4) | collective-permute-done | bytes 4587552 | tf_op jit(solution)/shard_map/ppermute | solution.py:102
  166.1 10.5 %fusion.51 = f32[1024,2560]{1,0:T(8,128)} fusion(bf16[1024,896]{1,0:T(8,128)(2,1)S(1)} %bitcast.143, bf16[896,2560]{1,0:T(8,128)(2,1)} %collective-permute-done.4), kind=kOutput, calls=%fused_computation.89 | convolution fusion | flops 4697620480 | bytes 16908288 | tf_op jit(solution)/shard_map/dot_general | solution.py:132
  176.6 10.6 %fusion.11 = f32[1024,2560]{1,0:T(8,128)} fusion(bf16[1024,896]{1,0:T(8,128)(2,1)S(1)} %bitcast.142, bf16[896,10240]{1,0:T(8,128)(2,1)} %param.8, s32[]{:T(128)S(6)} %select_n.78), kind=kOutput, calls=%fused_computation.19 | convolution fusion | flops 4697620480 | bytes 16908292 | tf_op jit(solution)/shard_map/dot_general | solution.py:132
  187.2 10.4 %fusion.50 = f32[1024,2560]{1,0:T(8,128)} fusion(bf16[1024,896]{1,0:T(8,128)(2,1)S(1)} %bitcast.141, bf16[896,2560]{1,0:T(8,128)(2,1)} %collective-permute-done.3), kind=kOutput, calls=%fused_computation.88 | convolution fusion | flops 4697620480 | bytes 16908288 | tf_op jit(solution)/shard_map/dot_general | solution.py:132
  197.5 83.0 %collective-permute-done.5 = bf16[896,2560]{1,0:T(8,128)(2,1)} collective-permute-done((bf16[896,2560]{1,0:T(8,128)(2,1)}, bf16[896,2560]{1,0:T(8,128)(2,1)}, u32[]{:S(2)}, u32[]{:S(2)}) %collective-permute-start.5) | collective-permute-done | bytes 4587552 | tf_op jit(solution)/shard_map/ppermute | solution.py:102
  280.5 18.3 %fusion.46 = (f32[1024]{0:T(1024)S(1)}, f32[1024,2560]{1,0:T(8,128)}) fusion(f32[1024,2560]{1,0:T(8,128)} %fusion.51, f32[1024,2560]{1,0:T(8,128)} %fusion.11, f32[1024,2560]{1,0:T(8,128)} %fusion.50, bf16[1024,896]{1,0:T(8,128)(2,1)S(1)} %bitcast.140, bf16[896,2560]{1,0:T(8,128)(2,1)} %collective-permute-done.5), kind=kOutput, calls=%fused_computation.84 | convolution fusion | flops 4708105216 | bytes 48369664 | tf_op jit(solution)/shard_map/dot_general | solution.py:132
  298.8 5.6 exponential_reduce_fusion
  304.5 8.3 %all-gather.5 = f32[4,2,1024]{2,1,0:T(2,128)S(1)} all-gather(f32[1,2,1024]{2,1,0:T(2,128)S(1)} %maximum_bitcast_fusion), channel_id=3, replica_groups=mesh['seq'=4,'vocab'=8] {'seq'}, dimensions={0}, use_global_device_ids=true | all-gather | bytes 40960 | tf_op jit(solution)/shard_map/all_gather | solution.py:140
  312.9 14.8 %all-gather.6 = f32[8,2,1024]{2,1,0:T(2,128)S(1)} all-gather(f32[1,2,1024]{2,1,0:T(2,128)S(1)} %maximum_bitcast_fusion.1), channel_id=4, replica_groups=mesh['seq'=4,'vocab'=8] {'vocab'}, dimensions={0}, use_global_device_ids=true | all-gather | bytes 73728 | tf_op jit(solution)/shard_map/all_gather | solution.py:140
  328.3 3.1 select_reduce_fusion
  331.4 2.0 fusion.8
  333.4 14.0 %all_gather.39 = f32[8,3,1024]{2,1,0:T(4,128)S(1)} all-gather(f32[1,3,1024]{2,1,0:T(4,128)S(1)} %pad_maximum_fusion.1), channel_id=1, replica_groups=mesh['seq'=4,'vocab'=8] {'vocab'}, dimensions={0}, use_global_device_ids=true | all-gather | bytes 110592 | tf_op jit(solution)/shard_map/all_gather | solution.py:153
  347.4 1.0 copy.51
  348.5 6.3 fusion.6
  354.8 4.4 fusion
  359.8 1.6 collective-permute-start.6
  361.3 113.3 %collective-permute-done.7.right_ref = bf16[1024,2560]{1,0:T(8,128)(2,1)S(1)} collective-permute-done((bf16[1024,2560]{1,0:T(8,128)(2,1)S(1)}, bf16[1024,2560]{1,0:T(8,128)(2,1)S(1)}, u32[]{:S(2)}, u32[]{:S(2)}) %collective-permute-start.7) | collective-permute-done | bytes 5242912 | tf_op jit(solution)/shard_map/ppermute | solution.py:102
  475.3 9.0 %fusion.9 = f32[1024,896]{1,0:T(8,128)S(1)} fusion(bf16[1024,2560]{1,0:T(8,128)(2,1)S(1)} %get-tuple-element.22.right_ref, bf16[896,10240]{1,0:T(8,128)(2,1)} %param.8, s32[]{:T(128)S(6)} %select_n.78), kind=kOutput, calls=%fused_computation.17 | convolution fusion | flops 4697620480 | bytes 13500420 | tf_op jit(solution)/shard_map/dot_general | solution.py:191
  485.0 10.9 %fusion.53 = f32[1024,896]{1,0:T(8,128)} fusion(bf16[1024,2560]{1,0:T(8,128)(2,1)S(1)} %collective-permute-done.7.right_ref, bf16[896,2560]{1,0:T(8,128)(2,1)} %get-tuple-element.24), kind=kOutput, calls=%fused_computation.91 | convolution fusion | flops 4697620480 | bytes 13500416 | tf_op jit(solution)/shard_map/dot_general | solution.py:191
  495.9 9.7 %fusion.52 = f32[1024,896]{1,0:T(8,128)} fusion(bf16[1024,2560]{1,0:T(8,128)(2,1)S(1)} %collective-permute-done.6.right_ref, bf16[896,2560]{1,0:T(8,128)(2,1)} %get-tuple-element.25), kind=kOutput, calls=%fused_computation.90 | convolution fusion | flops 4697620480 | bytes 13500416 | tf_op jit(solution)/shard_map/dot_general | solution.py:191
  505.6 27.5 %collective-permute-done.8 = bf16[512,2560]{1,0:T(8,128)(2,1)S(1)} collective-permute-done((bf16[512,2560]{1,0:T(8,128)(2,1)S(1)}, bf16[512,2560]{1,0:T(8,128)(2,1)S(1)}, u32[]{:S(2)}, u32[]{:S(2)}) %collective-permute-start.8) | collective-permute-done | bytes 2621472 | tf_op jit(solution)/shard_map/ppermute | solution.py:102
  533.3 9.6 %collective-permute-done.9 = bf16[512,2560]{1,0:T(8,128)(2,1)S(1)} collective-permute-done((bf16[512,2560]{1,0:T(8,128)(2,1)S(1)}, bf16[512,2560]{1,0:T(8,128)(2,1)S(1)}, u32[]{:S(2)}, u32[]{:S(2)}) %collective-permute-start.9) | collective-permute-done | bytes 2621472 | tf_op jit(solution)/shard_map/ppermute | solution.py:102
  543.1 2.7 copy-done.5
  545.7 1.1 copy-done.8
  546.8 10.4 %add_add_fusion.1 = f32[1024,896]{1,0:T(8,128)} fusion(f32[1024,896]{1,0:T(8,128)} %fusion.53, f32[1024,896]{1,0:T(8,128)S(1)} %fusion.9, f32[1024,896]{1,0:T(8,128)S(1)} %copy-done.8, bf16[1024,2560]{1,0:T(8,128)(2,1)S(1)} %constant_dynamic-update-slice_fusion.right_ref, bf16[896,2560]{1,0:T(8,128)(2,1)} %get-tuple-element.23), kind=kOutput, calls=%fused_computation.21 | convolution fusion | flops 4700372992 | bytes 24510464 | tf_op jit(solution)/shard_map/dot_general | solution.py:191
  557.2 9.3 %put_columns.4.rest_0_ = bf16[896,10240]{1,0:T(8,128)(2,1)} custom-call(s32[1]{0:T(128)} %bitcast.35.offset_ref, bf16[896,1024]{1,0:T(8,128)(2,1)} %bitcast.131, bf16[1024,2560]{1,0:T(8,128)(2,1)} %copy-done.2), custom_call_target="tpu_custom_call" | custom-call | flops 4697620480 | bytes 11665408 | tf_op jit(solution)/shard_map/put_columns/pallas_call | solution.py:69
  566.6 9.3 %put_columns.5.rest_0_ = bf16[896,10240]{1,0:T(8,128)(2,1)} custom-call(s32[1]{0:T(128)} %bitcast.34.offset_ref, bf16[896,1024]{1,0:T(8,128)(2,1)} %bitcast.132, bf16[1024,2560]{1,0:T(8,128)(2,1)} %copy-done.4, bf16[896,10240]{1,0:T(8,128)(2,1)} %put_columns.4.rest_0_), custom_call_target="tpu_custom_call", output_to_operand_aliasing={{}: (3, {})} | custom-call | flops 4697620480 | bytes 11665408 | tf_op jit(solution)/shard_map/put_columns/pallas_call | solution.py:69
  575.8 9.3 %put_columns.6.rest_0_ = bf16[896,10240]{1,0:T(8,128)(2,1)} custom-call(s32[1]{0:T(128)} %bitcast.33.offset_ref, bf16[896,1024]{1,0:T(8,128)(2,1)} %bitcast.133, bf16[1024,2560]{1,0:T(8,128)(2,1)} %copy-done.3, bf16[896,10240]{1,0:T(8,128)(2,1)} %put_columns.5.rest_0_), custom_call_target="tpu_custom_call", output_to_operand_aliasing={{}: (3, {})} | custom-call | flops 4697620480 | bytes 11665408 | tf_op jit(solution)/shard_map/put_columns/pallas_call | solution.py:69
  585.1 7.0 %all-gather.3 = f32[4096]{0:T(1024)S(1)} all-gather(f32[1024]{0:T(1024)S(1)} %get-tuple-element.12), channel_id=5, replica_groups=mesh['seq'=4,'vocab'=8] {'seq'}, dimensions={0}, use_global_device_ids=true | all-gather | bytes 20480 | tf_op jit(solution)/shard_map/all_gather | solution.py:201
  592.2 14.3 %all-gather.4 = f32[8192]{0:T(1024)S(1)} all-gather(f32[1024]{0:T(1024)S(1)} %reduce_sum.108), channel_id=6, replica_groups=mesh['seq'=4,'vocab'=8] {'vocab'}, dimensions={0}, use_global_device_ids=true | all-gather | bytes 36864 | tf_op jit(solution)/shard_map/all_gather | solution.py:201
  606.5 0.6 dynamic_slice.23
  607.1 9.2 %put_columns.7 = bf16[896,10240]{1,0:T(8,128)(2,1)} custom-call(s32[1]{0:T(128)} %bitcast.32.offset_ref, bf16[896,1024]{1,0:T(8,128)(2,1)} %bitcast.134, bf16[1024,2560]{1,0:T(8,128)(2,1)} %copy-done.5, bf16[896,10240]{1,0:T(8,128)(2,1)} %put_columns.6.rest_0_), custom_call_target="tpu_custom_call", output_to_operand_aliasing={{}: (3, {})} | custom-call | flops 4697620480 | bytes 11665408 | tf_op jit(solution)/shard_map/put_columns/pallas_call | solution.py:69
  616.4 1.7 convert_element_type.12
  (67 shorter events, 5.5 us)
Async XLA Ops:
  8.0 90.9 %all-gather.9.cloned.1.call-start = ((), (), s32[]{:S(2)}) async-start(), calls=%async_computation.3 | async-start | bytes 8257536 | tf_op jit(solution)/shard_map/all_gather | solution.py:114
  9.0 10.5 %collective-permute-start.2 = (bf16[128,896]{1,0:T(8,128)(2,1)S(1)}, bf16[128,896]{1,0:T(8,128)(2,1)S(1)}, u32[]{:S(2)}, u32[]{:S(2)}) collective-permute-start(bf16[128,896]{1,0:T(8,128)(2,1)S(1)} %constant_dynamic-slice_fusion), channel_id=1, source_target_pairs={{0,24},{8,16},{16,8},{24,0},{1,25},{9,17},{17,9},{25,1},{2,26},{10... | collective-permute-start | bytes 688136 | tf_op jit(solution)/shard_map/ppermute | solution.py:102
  13.0 10.5 %collective-permute-start.1 = (bf16[128,896]{1,0:T(8,128)(2,1)S(1)}, bf16[128,896]{1,0:T(8,128)(2,1)S(1)}, u32[]{:S(2)}, u32[]{:S(2)}) collective-permute-start(bf16[128,896]{1,0:T(8,128)(2,1)S(1)} %constant_dynamic-slice_fusion), channel_id=1, source_target_pairs={{0,16},{8,24},{16,0},{24,8},{1,17},{9,25},{17,1},{25,9},{2,18},{10... | collective-permute-start | bytes 688136 | tf_op jit(solution)/shard_map/ppermute | solution.py:102
  13.5 10.3 %collective-permute-start = (bf16[128,896]{1,0:T(8,128)(2,1)S(1)}, bf16[128,896]{1,0:T(8,128)(2,1)S(1)}, u32[]{:S(2)}, u32[]{:S(2)}) collective-permute-start(bf16[128,896]{1,0:T(8,128)(2,1)S(1)} %constant_dynamic-slice_fusion), channel_id=1, source_target_pairs={{0,8},{8,0},{16,24},{24,16},{1,9},{9,1},{17,25},{25,17},{2,10},{10... | collective-permute-start | bytes 688136 | tf_op jit(solution)/shard_map/ppermute | solution.py:102
  24.9 303.0 %all-reduce.2.cloned.1.call-start = ((), (), s32[]{:S(2)}) async-start(), calls=%async_computation.1 | async-start | bytes 8388608 | tf_op jit(solution)/shard_map/psum | solution.py:144
  25.0 13.8 %copy-start = (s32[8,64]{1,0:T(8,128)S(1)}, s32[8,64]{1,0:T(8,128)}, u32[]{:S(2)}) copy-start(s32[8,64]{1,0:T(8,128)} %param.9) | copy-start | bytes 6148
  35.3 5.3 copy-start.6
  35.3 130.8 %collective-permute-start.4 = (bf16[896,2560]{1,0:T(8,128)(2,1)}, bf16[896,2560]{1,0:T(8,128)(2,1)}, u32[]{:S(2)}, u32[]{:S(2)}) collective-permute-start(bf16[896,2560]{1,0:T(8,128)(2,1)} %get-tuple-element.24), channel_id=1, source_target_pairs={{0,16},{8,24},{16,0},{24,8},{1,17},{9,25},{17,1},{25,9},{2,18},{10... | collective-permute-start | bytes 13762568 | tf_op jit(solution)/shard_map/ppermute | solution.py:102
  36.6 150.5 %collective-permute-start.3 = (bf16[896,2560]{1,0:T(8,128)(2,1)}, bf16[896,2560]{1,0:T(8,128)(2,1)}, u32[]{:S(2)}, u32[]{:S(2)}) collective-permute-start(bf16[896,2560]{1,0:T(8,128)(2,1)} %get-tuple-element.25), channel_id=1, source_target_pairs={{0,8},{8,0},{16,24},{24,16},{1,9},{9,1},{17,25},{25,17},{2,10},{10... | collective-permute-start | bytes 13762568 | tf_op jit(solution)/shard_map/ppermute | solution.py:102
  37.2 243.4 %collective-permute-start.5 = (bf16[896,2560]{1,0:T(8,128)(2,1)}, bf16[896,2560]{1,0:T(8,128)(2,1)}, u32[]{:S(2)}, u32[]{:S(2)}) collective-permute-start(bf16[896,2560]{1,0:T(8,128)(2,1)} %get-tuple-element.23), channel_id=1, source_target_pairs={{0,24},{8,16},{16,8},{24,0},{1,25},{9,17},{17,9},{25,1},{2,26},{10... | collective-permute-start | bytes 13762568 | tf_op jit(solution)/shard_map/ppermute | solution.py:102
  91.6 524.8 %reduce-scatter.2.cloned.1.call-start = ((), (), s32[]{:S(2)}) async-start(), calls=%async_computation.2 | async-start | bytes 4128768 | tf_op jit(solution)/shard_map/reduce_scatter | solution.py:196
  327.9 3.5 copy-start.1
  333.3 15.2 %copy-start.7 = (s32[8,8]{1,0:T(8,128)S(1)}, s32[8,8]{1,0:T(8,128)}, u32[]{:S(2)}) copy-start(s32[8,8]{1,0:T(8,128)} %broadcast_clamp_fusion.ids_ref) | copy-start | bytes 772
  348.5 6.3 %slice-start = ((s8[10485760]{0:T(1024)(128)(4,1)}), s8[4194304]{0:T(1024)(128)(4,1)S(1)}, s32[]{:S(2)}) async-start(s8[10485760]{0:T(1024)(128)(4,1)} %bitcast.128), calls=%async_computation.4 | async-start | bytes 8388608
  348.5 6.3 %slice-start.1 = ((s8[10485760]{0:T(1024)(128)(4,1)}), s8[4194304]{0:T(1024)(128)(4,1)S(1)}, s32[]{:S(2)}) async-start(s8[10485760]{0:T(1024)(128)(4,1)} %bitcast.128), calls=%async_computation.5 | async-start | bytes 8388608
  348.5 6.3 %slice-start.2 = ((s8[10485760]{0:T(1024)(128)(4,1)}), s8[2097152]{0:T(1024)(128)(4,1)S(1)}, s32[]{:S(2)}) async-start(s8[10485760]{0:T(1024)(128)(4,1)} %bitcast.128), calls=%async_computation.6 | async-start | bytes 4194304
  359.2 125.1 %copy-start.2 = (bf16[1024,2560]{1,0:T(8,128)(2,1)}, bf16[1024,2560]{1,0:T(8,128)(2,1)S(1)}, u32[]{:S(2)}) copy-start(bf16[1024,2560]{1,0:T(8,128)(2,1)S(1)} %get-tuple-element.22.right_ref) | copy-start | bytes 15728644
  359.3 115.3 %collective-permute-start.7 = (bf16[1024,2560]{1,0:T(8,128)(2,1)S(1)}, bf16[1024,2560]{1,0:T(8,128)(2,1)S(1)}, u32[]{:S(2)}, u32[]{:S(2)}) collective-permute-start(bf16[1024,2560]{1,0:T(8,128)(2,1)S(1)} %get-tuple-element.22.right_ref), channel_id=1, source_target_pairs={{0,16},{8,24},{16,0},{24,8},{1,17},{9,25},{17,1},{25,9},{2,18},{10... | collective-permute-start | bytes 15728648 | tf_op jit(solution)/shard_map/ppermute | solution.py:102
  359.8 124.6 %collective-permute-start.6 = (bf16[1024,2560]{1,0:T(8,128)(2,1)S(1)}, bf16[1024,2560]{1,0:T(8,128)(2,1)S(1)}, u32[]{:S(2)}, u32[]{:S(2)}) collective-permute-start(bf16[1024,2560]{1,0:T(8,128)(2,1)S(1)} %get-tuple-element.22.right_ref), channel_id=1, source_target_pairs={{0,8},{8,0},{16,24},{24,16},{1,9},{9,1},{17,25},{25,17},{2,10},{10... | collective-permute-start | bytes 15728648 | tf_op jit(solution)/shard_map/ppermute | solution.py:102
  474.6 10.4 %copy-start.3 = (bf16[1024,2560]{1,0:T(8,128)(2,1)}, bf16[1024,2560]{1,0:T(8,128)(2,1)S(1)}, u32[]{:S(2)}) copy-start(bf16[1024,2560]{1,0:T(8,128)(2,1)S(1)} %collective-permute-done.7.right_ref) | copy-start | bytes 15728644
  474.8 58.3 %collective-permute-start.8 = (bf16[512,2560]{1,0:T(8,128)(2,1)S(1)}, bf16[512,2560]{1,0:T(8,128)(2,1)S(1)}, u32[]{:S(2)}, u32[]{:S(2)}) collective-permute-start(bf16[512,2560]{1,0:T(8,128)(2,1)S(1)} %slice.76), channel_id=1, source_target_pairs={{0,8},{8,0},{16,24},{24,16},{1,9},{9,1},{17,25},{25,17},{2,10},{10... | collective-permute-start | bytes 7864328 | tf_op jit(solution)/shard_map/ppermute | solution.py:102
  484.4 11.6 %copy-start.4 = (bf16[1024,2560]{1,0:T(8,128)(2,1)}, bf16[1024,2560]{1,0:T(8,128)(2,1)S(1)}, u32[]{:S(2)}) copy-start(bf16[1024,2560]{1,0:T(8,128)(2,1)S(1)} %collective-permute-done.6.right_ref) | copy-start | bytes 15728644
  484.5 58.3 %collective-permute-start.9 = (bf16[512,2560]{1,0:T(8,128)(2,1)S(1)}, bf16[512,2560]{1,0:T(8,128)(2,1)S(1)}, u32[]{:S(2)}, u32[]{:S(2)}) collective-permute-start(bf16[512,2560]{1,0:T(8,128)(2,1)S(1)} %slice.77), channel_id=1, source_target_pairs={{0,16},{8,24},{16,0},{24,8},{1,17},{9,25},{17,1},{25,9},{2,18},{10... | collective-permute-start | bytes 7864328 | tf_op jit(solution)/shard_map/ppermute | solution.py:102
  542.9 3.9 copy-start.8
  543.1 2.7 copy-start.5
Sparse Core Ops, SparseCore 0:
  25.0 73.8 all-gather.8
  557.3 45.2 reduce-scatter.1
Sparse Core Ops, SparseCore 1:
  91.6 217.9 all-reduce.1
